TPU v7x, 512 devices: a whole 4x4x16 slice. The times are simulated.
512 devices in a mesh: loop: 64 (over y_lo, z, core), grp: 8 (over x, y_hi).
Axes of the slice: x: 4, y: 4 (y_hi: 2, y_lo: 2; y = y_hi * 2 + y_lo), z: 16, core: 2. Of those that a mesh axis runs over, the one named last changes fastest.
Arguments:
- ratings: bfloat16 [2, 262144, 2048], P(None, ('loop', 'grp')), may hold values from -2.5 to 2.5, as said below
- user_factors: float32 [262144, 128], P(('loop', 'grp')), may hold values from -2 to 2
- user_accum: float32 [262144, 128], P(('loop', 'grp')), may hold values from 20 to 400
- item_factors: float32 [131072, 128], P('loop'), may hold values from -2 to 2
- item_accum: float32 [131072, 128], P('loop'), may hold values from 20 to 400
Outputs:
- users_out: float32 [262144, 128], P(('loop', 'grp'))
- items_out: float32 [131072, 128], P('loop')
Inputs may be any that keep to these rules, and one draw needn't show every extreme that they name: `ratings`: each entry is 0 (unobserved) or has magnitude 0.5 or more.
All inputs are finite; a program needn't handle non-finite values.
Results may differ from a plain program's by a relative error of at most 0.0085.
Values may be sent and summed in bfloat16 or wider, within the bound.
A program may use at most 64 MiB of HBM per device.

v0:
```python
import jax
import jax.numpy as jnp
from jax import lax
from jax.sharding import PartitionSpec as P

SUB = 2
INNER = 2
shrink = 0.05
learn_rate = 0.2
tiny_eps = 1e-06


def shifted(shard, axis, by):
    devices = lax.axis_size(axis)
    return lax.ppermute(shard, axis, [(i, (i + by) % devices) for i in range(devices)])


def adagrad(param, accum, grad):
    accum = accum + grad * grad
    return (param - learn_rate * grad / jnp.sqrt(accum + tiny_eps), accum)


def residual_terms(rate_full, observed, users, item_half):
    user_half = users.astype(jnp.bfloat16)
    predicted = lax.dot_general(
        user_half, item_half, (((1,), (1,)), ((), ())), preferred_element_type=jnp.float32
    )
    resid = (observed * (rate_full - predicted)).astype(jnp.bfloat16)
    grad_user = -jnp.dot(resid, item_half, preferred_element_type=jnp.float32) + shrink * users
    return (user_half, resid, grad_user)


def local(ratings, user_factors, user_accum, item_factors, item_accum):
    users = user_factors
    user_acc = user_accum
    items = item_factors
    item_acc = item_accum
    for sub_epoch in range(SUB):
        if sub_epoch > 0:
            items, item_acc = shifted((items, item_acc), "loop", 1)
        rate_full = ratings[sub_epoch].astype(jnp.float32)
        observed = (jnp.abs(rate_full) > 0.25).astype(jnp.float32)
        for inner_step in range(INNER):
            item_half = items.astype(jnp.bfloat16)
            user_half, resid, grad_user = residual_terms(rate_full, observed, users, item_half)
            own_term = -lax.dot_general(
                resid, user_half, (((0,), (0,)), ((), ())), preferred_element_type=jnp.float32
            )
            grad_item = (
                lax.psum(own_term.astype(jnp.bfloat16), "grp").astype(jnp.float32) + shrink * items
            )
            users, user_acc = adagrad(users, user_acc, grad_user)
            items, item_acc = adagrad(items, item_acc, grad_item)
    return (users, items)


def solution(mesh):
    in_specs = (
        P(None, ("loop", "grp"), None),
        P(("loop", "grp"), None),
        P(("loop", "grp"), None),
        P("loop", None),
        P("loop", None),
    )
    out_specs = (P(("loop", "grp"), None), P("loop", None))
    return jax.shard_map(local, mesh=mesh, in_specs=in_specs, out_specs=out_specs, check_vma=False)
```

profile of v0, /device:TPU:32, one launch (start us, length us, event | category | flops | bytes accessed | tf_op | source)
XLA Modules:
  0.0 459.4 jit_solution(7370954499293579164)
XLA Ops:
  7.2 0.0 all-reduce.5.cloned.1.call-start
  7.2 0.0 copy-start.6
  7.2 3.0 fusion.2
  10.2 0.0 copy-done.6
  10.3 0.0 copy-start
  10.3 0.0 copy-start.5
  10.3 1.6 fusion.10
  11.8 0.0 all-reduce.5.cloned.1.call-update
  11.9 0.0 all-reduce.7.cloned.1.call-start
  11.9 0.0 copy-done
  11.9 0.0 copy-done.5
  11.9 2.5 multiply_subtract_fusion.7
  14.4 103.1 %all-reduce.5.cloned.1.call-done = bf16[2048,128]{1,0:T(8,128)(2,1)} async-done(((bf16[2048,128]{1,0:T(8,128)(2,1)}), bf16[2048,128]{1,0:T(8,128)(2,1)}) %all-reduce.5.cloned.1.call-update) | async-done | bytes 524304 | tf_op jit(solution)/shard_map/psum | solution.py:50
  117.5 0.0 copy-start.3
  117.5 3.4 fusion.4
  120.9 0.0 copy-done.3
  120.9 1.6 fusion.11
  122.5 0.0 all-reduce.7.cloned.1.call-update
  122.5 0.0 all-reduce.9.cloned.1.call-start
  122.5 99.3 %all-reduce.7.cloned.1.call-done = bf16[2048,128]{1,0:T(8,128)(2,1)} async-done(((bf16[2048,128]{1,0:T(8,128)(2,1)}), bf16[2048,128]{1,0:T(8,128)(2,1)}) %all-reduce.7.cloned.1.call-update) | async-done | bytes 524304 | tf_op jit(solution)/shard_map/psum | solution.py:50
  221.8 0.0 copy-start.1
  221.8 0.0 copy-start.2
  221.8 3.3 multiply_add_fusion.2
  225.1 1.9 collective-permute-start
  227.0 0.0 copy-done.1
  227.0 0.0 copy-done.2
  227.1 0.0 copy-done.4
  227.1 0.0 copy-start.8
  227.1 2.8 multiply_subtract_fusion.6
  229.9 3.6 collective-permute-start.1
  233.4 7.8 %collective-permute-done = f32[2048,128]{1,0:T(8,128)S(1)} collective-permute-done((f32[2048,128]{1,0:T(8,128)S(1)}, f32[2048,128]{1,0:T(8,128)S(1)}, u32[]{:S(2)}, u32[]{:S(2)}) %collective-permute-start) | collective-permute-done | bytes 1048608 | tf_op jit(solution)/shard_map/ppermute | solution.py:15
  241.2 0.0 copy-done.8
  241.2 1.0 fusion.7
  242.3 1.6 fusion.12
  243.8 0.0 all-reduce.9.cloned.1.call-update
  243.9 0.2 all-reduce.11.cloned.1.call-start
  244.1 2.4 fusion.25
  246.5 6.1 %collective-permute-done.1 = f32[2048,128]{1,0:T(8,128)} collective-permute-done((f32[2048,128]{1,0:T(8,128)}, f32[2048,128]{1,0:T(8,128)}, u32[]{:S(2)}, u32[]{:S(2)}) %collective-permute-start.1) | collective-permute-done | bytes 1048608 | tf_op jit(solution)/shard_map/ppermute | solution.py:15
  252.6 91.8 %all-reduce.9.cloned.1.call-done = bf16[2048,128]{1,0:T(8,128)(2,1)} async-done(((bf16[2048,128]{1,0:T(8,128)(2,1)}), bf16[2048,128]{1,0:T(8,128)(2,1)}) %all-reduce.9.cloned.1.call-update) | async-done | bytes 524304 | tf_op jit(solution)/shard_map/psum | solution.py:50
  344.4 1.7 fusion.18
  346.1 0.0 copy-start.7
  346.1 2.7 fusion.9
  348.8 0.0 copy-done.7
  348.9 1.6 fusion.13
  350.4 0.0 all-reduce.11.cloned.1.call-update
  350.5 2.6 multiply_subtract_fusion.4
  353.1 96.6 %all-reduce.11.cloned.1.call-done = bf16[2048,128]{1,0:T(8,128)(2,1)} async-done(((bf16[2048,128]{1,0:T(8,128)(2,1)}), bf16[2048,128]{1,0:T(8,128)(2,1)}) %all-reduce.11.cloned.1.call-update) | async-done | bytes 524304 | tf_op jit(solution)/shard_map/psum | solution.py:50
  449.7 3.2 multiply_subtract_fusion
  (1 shorter events, 0.0 us)
Async XLA Ops:
  7.2 110.3 %all-reduce.5.cloned.1.call-start = ((), (), s32[]{:S(2)}) async-start(), calls=%async_computation | async-start | bytes 1048576 | tf_op jit(solution)/shard_map/psum | solution.py:50
  7.2 3.0 copy-start.6
  10.3 1.7 copy-start
  10.3 1.7 copy-start.5
  11.9 209.9 %all-reduce.7.cloned.1.call-start = ((), (), s32[]{:S(2)}) async-start(), calls=%async_computation.1 | async-start | bytes 1048576 | tf_op jit(solution)/shard_map/psum | solution.py:50
  117.5 3.4 copy-start.3
  122.5 221.9 %all-reduce.9.cloned.1.call-start = ((), (), s32[]{:S(2)}) async-start(), calls=%async_computation.2 | async-start | bytes 1048576 | tf_op jit(solution)/shard_map/psum | solution.py:50
  221.8 5.2 %copy-start.1 = (f32[2048,128]{1,0:T(8,128)S(1)}, f32[2048,128]{1,0:T(8,128)}, u32[]{:S(2)}) copy-start(f32[2048,128]{1,0:T(8,128)} %param.8) | copy-start | bytes 3145732
  221.8 5.2 %copy-start.2 = (f32[2048,128]{1,0:T(8,128)S(1)}, f32[2048,128]{1,0:T(8,128)}, u32[]{:S(2)}) copy-start(f32[2048,128]{1,0:T(8,128)} %param.9) | copy-start | bytes 3145732
  221.8 5.3 %copy-start.4 = (bf16[2048,128]{1,0:T(8,128)(2,1)S(1)}, bf16[2048,128]{1,0:T(8,128)(2,1)}, u32[]{:S(2)}) copy-start(bf16[2048,128]{1,0:T(8,128)(2,1)} %all-reduce.5.cloned.1.call-done) | copy-start | bytes 1572868
  225.1 16.1 %collective-permute-start = (f32[2048,128]{1,0:T(8,128)S(1)}, f32[2048,128]{1,0:T(8,128)S(1)}, u32[]{:S(2)}, u32[]{:S(2)}) collective-permute-start(f32[2048,128]{1,0:T(8,128)S(1)} %get-tuple-element.5), channel_id=1, source_target_pairs={{0,8},{8,16},{16,24},{24,32},{32,40},{40,48},{48,56},{56,64},{64,7... | collective-permute-start | bytes 3145736 | tf_op jit(solution)/shard_map/ppermute | solution.py:15
  227.1 14.2 %copy-start.8 = (bf16[2,512,2048]{2,1,0:T(8,128)(2,1)S(1)}, bf16[2,512,2048]{2,1,0:T(8,128)(2,1)}, u32[]{:S(2)}) copy-start(bf16[2,512,2048]{2,1,0:T(8,128)(2,1)} %param.5) | copy-start | bytes 12582916
  229.9 22.7 %collective-permute-start.1 = (f32[2048,128]{1,0:T(8,128)}, f32[2048,128]{1,0:T(8,128)}, u32[]{:S(2)}, u32[]{:S(2)}) collective-permute-start(f32[2048,128]{1,0:T(8,128)} %get-tuple-element.4), channel_id=1, source_target_pairs={{0,8},{8,16},{16,24},{24,32},{32,40},{40,48},{48,56},{56,64},{64,7... | collective-permute-start | bytes 3145736 | tf_op jit(solution)/shard_map/ppermute | solution.py:15
  243.9 205.9 %all-reduce.11.cloned.1.call-start = ((), (), s32[]{:S(2)}) async-start(), calls=%async_computation.3 | async-start | bytes 1048576 | tf_op jit(solution)/shard_map/psum | solution.py:50
  346.1 2.7 copy-start.7
Sparse Core Ops, SparseCore 0:
  12.0 105.4 all-reduce.4
  122.6 99.1 all-reduce.6
  244.0 100.3 all-reduce.8
  350.6 99.0 all-reduce.10
where the time goes:
time: 460 us; the launch traced here: 459 us
  waiting for transfers between devices  405 us (88%)
  matrix products  26.7 us (6%)
  between operations  13.9 us (3%)
  other arithmetic  8.22 us (2%)
  starting transfers between devices  5.81 us (1%)
    psum x4, waiting for transfers between devices, local(): lax.psum(own_term.astype(jnp.bfloat16), 'grp').astype(jnp.float32)  391 us
    ppermute x2, waiting for transfers between devices, shifted(): lax.ppermute(shard, axis, [(i, (i + by) % devices) for i in range(devices)])  13.9 us
    dot_general x4, matrix products, residual_terms(): jnp.dot(resid, item_half, preferred_element_type=jnp.float32)  10.3 us
    dot_general x4, matrix products, residual_terms(): lax.dot_general(user_half, item_half, (((1,), (1,)), ((), ())), preferred...  10.2 us
  transfers between devices with their start and end apart: 6, of which 6 were waited for; matrix products, arithmetic and copies ran while one was open for 3% of the time, Pallas kernels for 0%

commit v1 on v0

--- a/solution.py
+++ b/solution.py
@@ -47,7 +47,10 @@
                 resid, user_half, (((0,), (0,)), ((), ())), preferred_element_type=jnp.float32
             )
             grad_item = (
-                lax.psum(own_term.astype(jnp.bfloat16), "grp").astype(jnp.float32) + shrink * items
+                jnp.sum(lax.all_gather(own_term.astype(jnp.bfloat16), "grp"), axis=0).astype(
+                    jnp.float32
+                )
+                + shrink * items
             )
             users, user_acc = adagrad(users, user_acc, grad_user)
             items, item_acc = adagrad(items, item_acc, grad_item)

time: 460 us -> 418 us (0.909)
  the two profiles are of different devices: /device:TPU:32 before, /device:TPU:1 now
where the time goes in v1:
time: 418 us; the launch traced here: 417 us
  waiting for transfers between devices  346 us (83%)
  matrix products  25.1 us (6%)
  other arithmetic  21.5 us (5%)
  between operations  14 us (3%)
  starting transfers between devices  9.45 us (2%)
    all_gather x4, waiting for transfers between devices, local(): lax.all_gather(own_term.astype(jnp.bfloat16), 'grp')  336 us
    reduce_sum x4, other arithmetic, local(): jnp.sum(lax.all_gather(own_term.astype(jnp.bfloat16), 'grp'), axis=0)  13.5 us
    ppermute x2, waiting for transfers between devices, shifted(): lax.ppermute(shard, axis, [(i, (i + by) % devices) for i in range(devices)])  10.1 us
    dot_general x4, matrix products, residual_terms(): lax.dot_general(user_half, item_half, (((1,), (1,)), ((), ())), preferred...  9.87 us
    ppermute x2, starting transfers between devices, shifted(): lax.ppermute(shard, axis, [(i, (i + by) % devices) for i in range(devices)])  9.29 us
    dot_general x4, matrix products, residual_terms(): jnp.dot(resid, item_half, preferred_element_type=jnp.float32)  8.98 us
  transfers between devices with their start and end apart: 6, of which 5 were waited for; matrix products, arithmetic and copies ran while one was open for 3% of the time, Pallas kernels for 0%

profile of v1, /device:TPU:1, one launch (start us, length us, event | category | flops | bytes accessed | tf_op | source)
XLA Modules:
  0.0 417.1 jit_solution(15496833185395703203)
XLA Ops:
  7.2 0.0 copy-start.10
  7.2 0.0 all-gather.9.cloned.1.call-start
  7.2 3.0 fusion.2
  10.2 0.0 copy-done.10
  10.2 0.0 copy-start
  10.3 1.6 fusion.10
  11.8 0.0 all-gather.9.cloned.1.call-update
  11.8 0.0 all-gather.11.cloned.1.call-start
  11.9 0.0 copy-done
  11.9 2.4 multiply_subtract_fusion.7
  14.4 89.2 %all-gather.9.cloned.1.call-done = bf16[16384,128]{1,0:T(8,128)(2,1)} async-done(((bf16[2048,128]{1,0:T(8,128)(2,1)}), bf16[16384,128]{1,0:T(8,128)(2,1)}) %all-gather.9.cloned.1.call-update) | async-done | bytes 4194320 | tf_op jit(solution)/shard_map/all_gather | solution.py:50
  103.6 3.7 reduce_sum.48
  107.3 3.3 fusion.4
  110.6 1.6 fusion.11
  112.1 0.0 all-gather.11.cloned.1.call-update
  112.2 0.0 all-gather.13.cloned.1.call-start
  112.2 85.1 %all-gather.11.cloned.1.call-done = bf16[16384,128]{1,0:T(8,128)(2,1)} async-done(((bf16[2048,128]{1,0:T(8,128)(2,1)}), bf16[16384,128]{1,0:T(8,128)(2,1)}) %all-gather.11.cloned.1.call-update) | async-done | bytes 4194320 | tf_op jit(solution)/shard_map/all_gather | solution.py:50
  197.3 3.7 reduce_sum.49
  201.0 0.0 copy-start.9
  201.0 3.3 multiply_add_fusion.2
  204.3 4.7 %collective-permute-start = (f32[2048,128]{1,0:T(8,128)S(1)}, f32[2048,128]{1,0:T(8,128)S(1)}, u32[]{:S(2)}, u32[]{:S(2)}) collective-permute-start(f32[2048,128]{1,0:T(8,128)S(1)} %get-tuple-element.5), channel_id=1, source_target_pairs={{0,8},{8,16},{16,24},{24,32},{32,40},{40,48},{48,56},{56,64},{64,7... | collective-permute-start | bytes 3145736 | tf_op jit(solution)/shard_map/ppermute | solution.py:15
  209.1 0.0 copy-done.1
  209.1 0.0 copy-done.4
  209.1 0.0 copy-done.5
  209.1 0.0 copy-done.7
  209.1 0.0 copy-done.8
  209.1 0.0 copy-done.9
  209.1 1.5 multiply_subtract_fusion.6
  210.6 10.1 %collective-permute-done = f32[2048,128]{1,0:T(8,128)S(1)} collective-permute-done((f32[2048,128]{1,0:T(8,128)S(1)}, f32[2048,128]{1,0:T(8,128)S(1)}, u32[]{:S(2)}, u32[]{:S(2)}) %collective-permute-start) | collective-permute-done | bytes 1048608 | tf_op jit(solution)/shard_map/ppermute | solution.py:15
  220.8 1.0 fusion.7
  221.8 1.6 fusion.12
  223.4 0.0 all-gather.13.cloned.1.call-update
  223.4 0.0 all-gather.15.cloned.1.call-start
  223.5 4.6 %collective-permute-start.1 = (f32[2048,128]{1,0:T(8,128)}, f32[2048,128]{1,0:T(8,128)}, u32[]{:S(2)}, u32[]{:S(2)}) collective-permute-start(f32[2048,128]{1,0:T(8,128)} %get-tuple-element.4), channel_id=1, source_target_pairs={{0,8},{8,16},{16,24},{24,32},{32,40},{40,48},{48,56},{56,64},{64,7... | collective-permute-start | bytes 3145736 | tf_op jit(solution)/shard_map/ppermute | solution.py:15
  228.1 2.4 fusion.25
  230.4 79.3 %all-gather.13.cloned.1.call-done = bf16[16384,128]{1,0:T(8,128)(2,1)} async-done(((bf16[2048,128]{1,0:T(8,128)(2,1)}), bf16[16384,128]{1,0:T(8,128)(2,1)}) %all-gather.13.cloned.1.call-update) | async-done | bytes 4194320 | tf_op jit(solution)/shard_map/all_gather | solution.py:50
  309.7 3.1 reduce_sum.50
  312.8 0.0 collective-permute-done.1
  312.8 1.8 fusion.18
  314.6 0.0 copy-start.11
  314.6 0.8 copy-done.11
  315.4 2.5 fusion.9
  317.9 1.6 fusion.13
  319.5 0.0 all-gather.15.cloned.1.call-update
  319.5 2.6 multiply_subtract_fusion.4
  322.1 82.5 %all-gather.15.cloned.1.call-done = bf16[16384,128]{1,0:T(8,128)(2,1)} async-done(((bf16[2048,128]{1,0:T(8,128)(2,1)}), bf16[16384,128]{1,0:T(8,128)(2,1)}) %all-gather.15.cloned.1.call-update) | async-done | bytes 4194320 | tf_op jit(solution)/shard_map/all_gather | solution.py:50
  404.6 3.1 reduce_sum.51
  407.7 2.9 multiply_subtract_fusion
  (13 shorter events, 0.0 us)
Async XLA Ops:
  7.2 3.1 copy-start.10
  7.2 96.4 %all-gather.9.cloned.1.call-start = ((), (), s32[]{:S(2)}) async-start(), calls=%async_computation | async-start | bytes 4718592 | tf_op jit(solution)/shard_map/all_gather | solution.py:50
  10.2 1.7 copy-start
  11.8 185.4 %all-gather.11.cloned.1.call-start = ((), (), s32[]{:S(2)}) async-start(), calls=%async_computation.1 | async-start | bytes 4718592 | tf_op jit(solution)/shard_map/all_gather | solution.py:50
  14.4 96.2 %copy-start.6 = (f32[512,128]{1,0:T(8,128)}, f32[512,128]{1,0:T(8,128)S(1)}, u32[]{:S(2)}) copy-start(f32[512,128]{1,0:T(8,128)S(1)} %get-tuple-element.6) | copy-start | bytes 786436
  112.2 197.6 %all-gather.13.cloned.1.call-start = ((), (), s32[]{:S(2)}) async-start(), calls=%async_computation.2 | async-start | bytes 4718592 | tf_op jit(solution)/shard_map/all_gather | solution.py:50
  201.0 8.1 %copy-start.1 = (f32[2048,128]{1,0:T(8,128)S(1)}, f32[2048,128]{1,0:T(8,128)}, u32[]{:S(2)}) copy-start(f32[2048,128]{1,0:T(8,128)} %param.8) | copy-start | bytes 3145732
  201.0 8.1 %copy-start.4 = (bf16[2048,128]{1,0:T(8,128)(2,1)S(1)}, bf16[2048,128]{1,0:T(8,128)(2,1)}, u32[]{:S(2)}) copy-start(bf16[2048,128]{1,0:T(8,128)(2,1)} %reduce_sum.48) | copy-start | bytes 1572868
  201.0 8.1 %copy-start.5 = (f32[2048,128]{1,0:T(8,128)S(1)}, f32[2048,128]{1,0:T(8,128)}, u32[]{:S(2)}) copy-start(f32[2048,128]{1,0:T(8,128)} %param.9) | copy-start | bytes 3145732
  201.0 8.1 %copy-start.7 = (f32[512,128]{1,0:T(8,128)S(1)}, f32[512,128]{1,0:T(8,128)}, u32[]{:S(2)}) copy-start(f32[512,128]{1,0:T(8,128)} %copy-done.6) | copy-start | bytes 786436
  201.0 8.1 %copy-start.8 = (f32[512,128]{1,0:T(8,128)S(1)}, f32[512,128]{1,0:T(8,128)}, u32[]{:S(2)}) copy-start(f32[512,128]{1,0:T(8,128)} %param.7) | copy-start | bytes 786436
  201.0 8.1 %copy-start.9 = (f32[512,128]{1,0:T(8,128)S(1)}, f32[512,128]{1,0:T(8,128)}, u32[]{:S(2)}) copy-start(f32[512,128]{1,0:T(8,128)} %get-tuple-element.7) | copy-start | bytes 786436
  204.3 16.5 %copy-start.12 = (bf16[2,512,2048]{2,1,0:T(8,128)(2,1)S(1)}, bf16[2,512,2048]{2,1,0:T(8,128)(2,1)}, u32[]{:S(2)}) copy-start(bf16[2,512,2048]{2,1,0:T(8,128)(2,1)} %param.5) | copy-start | bytes 12582916
  204.3 16.4 %collective-permute-start = (f32[2048,128]{1,0:T(8,128)S(1)}, f32[2048,128]{1,0:T(8,128)S(1)}, u32[]{:S(2)}, u32[]{:S(2)}) collective-permute-start(f32[2048,128]{1,0:T(8,128)S(1)} %get-tuple-element.5), channel_id=1, source_target_pairs={{0,8},{8,16},{16,24},{24,32},{32,40},{40,48},{48,56},{56,64},{64,7... | collective-permute-start | bytes 3145736 | tf_op jit(solution)/shard_map/ppermute | solution.py:15
  223.4 181.2 %all-gather.15.cloned.1.call-start = ((), (), s32[]{:S(2)}) async-start(), calls=%async_computation.3 | async-start | bytes 4718592 | tf_op jit(solution)/shard_map/all_gather | solution.py:50
  223.5 89.3 %collective-permute-start.1 = (f32[2048,128]{1,0:T(8,128)}, f32[2048,128]{1,0:T(8,128)}, u32[]{:S(2)}, u32[]{:S(2)}) collective-permute-start(f32[2048,128]{1,0:T(8,128)} %get-tuple-element.4), channel_id=1, source_target_pairs={{0,8},{8,16},{16,24},{24,32},{32,40},{40,48},{48,56},{56,64},{64,7... | collective-permute-start | bytes 3145736 | tf_op jit(solution)/shard_map/ppermute | solution.py:15
  312.8 1.8 copy-start.2
  314.6 0.8 copy-start.11
  322.1 85.6 %copy-start.3 = (bf16[2048,128]{1,0:T(8,128)(2,1)S(1)}, bf16[2048,128]{1,0:T(8,128)(2,1)}, u32[]{:S(2)}) copy-start(bf16[2048,128]{1,0:T(8,128)(2,1)} %copy-done.2) | copy-start | bytes 1572868
Sparse Core Ops, SparseCore 0:
  12.0 91.5 all-gather.8
  112.3 84.9 all-gather.10
  223.6 86.1 all-gather.12
  319.6 84.9 all-gather.14
